TPU v7x, 32 devices: a whole 2x2x4 slice. The times are simulated.
32 devices in a mesh: grp: 2 (over y), row: 4 (over z), col: 2 (over x), half: 2 (over core).
Axes of the slice: x: 2, y: 2, z: 4, core: 2. Of those that a mesh axis runs over, the one named last changes fastest.
Arguments:
- vecs: bfloat16 [4, 1024, 32768], P(('grp', 'half'), 'row', 'col'), parts along dimension 0, may hold values from -6 to 6
- poles: float32 [4, 32768], P(('grp', 'half'), 'col'), parts along dimension 0, may hold values from -512 to 512, as said below
- weights: float32 [4, 32768], P(('grp', 'half'), 'col'), parts along dimension 0, may hold values from -5 to 5
- kept: int32 [4, 32768], P(('grp', 'half'), 'col'), parts along dimension 0, may hold values 0 or 1
- roots: float32 [1024], P(('grp', 'row')), parts along dimension 0, may hold values from -512 to 512, as said below
- order: int32 [1024], P('grp'), parts along dimension 0, may hold values from 0 to 511, each once
Outputs:
- merged: bfloat16 [16, 4, 2, 32, 512], P(('grp', 'row', 'half'), None, None, None, 'col'), parts along dimension 0
There are 2 independent parts, one for each index of `grp`. A program takes and returns all parts, laid end to end along the dimension named above; each array names one. Nothing has to cross between parts.
Inputs may be any that keep to these rules, and one draw needn't show every extreme that they name: `poles`: every root differs from every pole by 0.2 or more. `roots`: every root differs from every pole by 0.2 or more. `order`: A permutation of 0 to 511.
All inputs are finite; a program needn't handle non-finite values. No bound on the sum of `kept` on one device may be relied on, other than what follows from the above.
Results may differ from a plain program's by a relative error of at most 0.0049.
Values may be sent and summed in bfloat16 or wider, within the bound.
A program may use at most 64 MiB of HBM per device.

v0:
```python
import jax
import jax.numpy as jnp
from jax import lax
from jax.sharding import PartitionSpec as P


def cauchy_block(scaled, centers, theta):
    return scaled[:, None] / (centers[:, None] - theta[None, :])


def body(vecs, poles, weights, kept, roots, order):
    all_roots = lax.all_gather(roots, "row", axis=0, tiled=True)
    width = all_roots.shape[0]
    picks = (order[:, None] == jnp.arange(width, dtype=jnp.int32)[None, :]).astype(jnp.float32)
    theta = jnp.dot(picks, all_roots, precision=lax.Precision.HIGHEST)
    scaled = (weights * kept.astype(jnp.float32))[0]
    centers = poles[0]
    plane = vecs[0]
    nrows = plane.shape[0]
    share_cols = width // lax.axis_size("col")
    cauchy = cauchy_block(scaled, centers, theta)
    norms = lax.psum(jnp.sum(cauchy * cauchy, axis=0), ("col", "half"))
    zpanel = (cauchy * lax.rsqrt(norms + 1e-06)).astype(jnp.bfloat16)
    share = lax.psum_scatter(
        lax.dot_general(
            zpanel, plane, (((0,), (1,)), ((), ())), preferred_element_type=jnp.float32
        ),
        "col",
        scatter_dimension=0,
        tiled=True,
    )
    block = jnp.transpose(share.astype(jnp.bfloat16))
    row_count = lax.axis_size("row")
    halves = lax.axis_size("half")
    groups = row_count * halves
    depth = nrows // groups
    pieces = block.reshape(groups, depth, share_cols)
    moved = lax.all_to_all(pieces, ("row", "half"), split_axis=0, concat_axis=0, tiled=True)
    return moved.reshape(1, row_count, halves, depth, share_cols)


def solution(mesh):
    return jax.shard_map(
        body,
        mesh=mesh,
        in_specs=(
            P(("grp", "half"), "row", "col"),
            P(("grp", "half"), "col"),
            P(("grp", "half"), "col"),
            P(("grp", "half"), "col"),
            P(("grp", "row")),
            P("grp"),
        ),
        out_specs=P(("grp", "row", "half"), None, None, None, "col"),
        check_vma=False,
    )
```

profile of v0, /device:TPU:0, one launch (start us, length us, event | category | flops | bytes accessed | tf_op | source)
XLA Modules:
  0.0 88.0 jit_solution(14186883042539817285)
XLA Ops:
  6.5 0.0 reduce-scatter.2.cloned.1.call-start
  6.5 12.8 %all-gather = f32[4,1,128]{2,1,0:T(1,128)S(1)} all-gather(f32[1,1,128]{2,1,0:T(1,128)} %bitcast.24), channel_id=1, replica_groups=mesh['grp'=2,'row'=4,'col'=2,'half'=2] {'row'}, dimensions={0}, use_global_device_ids=true | all-gather | bytes 2560 | tf_op jit(solution)/shard_map/all_gather | solution.py:12
  19.3 1.3 %fusion.2 = f32[1,512]{1,0:T(1,128)S(1)} fusion(s32[512]{0:T(512)} %param.11, f32[4,1,128]{2,1,0:T(1,128)S(1)} %all-gather), kind=kOutput, calls=%fused_computation.6 | convolution fusion | flops 3407872 | bytes 6144 | tf_op jit(solution)/shard_map/dot_general | solution.py:15
  20.6 1.0 %convert_multiply_fusion = f32[1,16384]{1,0:T(1,128)S(1)} fusion(f32[1,16384]{1,0:T(1,128)} %param.8, s32[1,16384]{1,0:T(1,128)} %param.9), kind=kLoop, calls=%fused_computation.9 | loop fusion | flops 32768 | bytes 196608 | tf_op jit(solution)/shard_map/mul | solution.py:16
  21.6 13.8 %multiply_reduce_fusion = f32[512]{0:T(512)S(1)} fusion(f32[512]{0:T(512)S(1)} %bitcast.22, f32[16384]{0:T(1024)} %bitcast.20, f32[16384]{0:T(1024)S(1)} %bitcast.18), kind=kLoop, calls=%fused_computation.1 | loop fusion | flops 33553920 | bytes 135168 | tf_op jit(solution)/shard_map/reduce_sum | solution.py:22
  35.4 5.7 %psum.7 = f32[512]{0:T(512)S(1)} all-reduce(f32[512]{0:T(512)S(1)} %multiply_reduce_fusion), channel_id=1, replica_groups=mesh['grp'=2,'row'=4,'col'=2,'half'=2] {'col','half'}, use_global_device_ids=true, to_apply=%region_1.0 | all-reduce | flops 512 | bytes 4096 | tf_op jit(solution)/shard_map/psum | solution.py:22
  41.1 13.9 %fusion = f32[512,256]{1,0:T(8,128)} fusion(f32[512]{0:T(512)S(1)} %add_rsqrt_fusion, f32[512]{0:T(512)S(1)} %bitcast.23, f32[16384]{0:T(1024)} %bitcast.21, f32[16384]{0:T(1024)S(1)} %bitcast.19, bf16[1,256,16384]{2,1,0:T(8,128)(2,1)} %param.6), kind=kOutput, calls=%fused_computation.3 | convolution fusion | flops 4328521728 | bytes 9048064 | tf_op jit(solution)/shard_map/dot_general | solution.py:25
  55.0 0.0 reduce-scatter.2.cloned.1.call-update
  55.0 13.2 %reduce-scatter.2.cloned.1.call-done = f32[256,256]{1,0:T(8,128)} async-done(((f32[512,256]{1,0:T(8,128)}), f32[256,256]{1,0:T(8,128)}) %reduce-scatter.2.cloned.1.call-update) | async-done | bytes 262160 | tf_op jit(solution)/shard_map/reduce_scatter | solution.py:24
  68.2 1.0 %convert_bitcast_fusion = bf16[256,256]{0,1:T(8,128)(2,1)S(1)} fusion(f32[256,256]{1,0:T(8,128)} %reduce-scatter.2.cloned.1.call-done), kind=kLoop, calls=%fused_computation.8 | loop fusion | flops 65536 | bytes 393216 | tf_op jit(solution)/shard_map/transpose | solution.py:32
  69.2 0.1 copy.10
  69.3 11.2 %all_to_all.5 = bf16[8,32,256]{2,1,0:T(8,128)(2,1)S(1)} all-to-all(bf16[8,32,256]{2,1,0:T(8,128)(2,1)S(1)} %bitcast.16), channel_id=1, replica_groups=mesh['grp'=2,'row'=4,'col'=2,'half'=2] {'row','half'}, dimensions={0} | all-to-all | bytes 262144 | tf_op jit(solution)/shard_map/all_to_all | solution.py:38
  80.5 0.7 copy.12
  (1 shorter events, 0.0 us)
Async XLA Ops:
  6.5 61.7 %reduce-scatter.2.cloned.1.call-start = ((), (), s32[]{:S(2)}) async-start(), calls=%async_computation.2 | async-start | bytes 786432 | tf_op jit(solution)/shard_map/reduce_scatter | solution.py:24
Sparse Core Ops, SparseCore 0:
  55.1 13.0 reduce-scatter.1
where the time goes:
time: 88.3 us; the launch traced here: 88 us
  blocking collectives  29.6 us (34%)
  other arithmetic  15.7 us (18%)
  matrix products  15.2 us (17%)
  between operations  13.4 us (15%)
  waiting for transfers between devices  13.2 us (15%)
    dot_general x1, matrix products, body(): lax.dot_general(zpanel, plane, (((0,), (1,)), ((), ())), preferred_elemen...  13.9 us
    reduce_sum x1, other arithmetic, body(): norms = lax.psum(jnp.sum(cauchy * cauchy, axis=0), ('col', 'half'))  13.8 us
    reduce_scatter x1, waiting for transfers between devices, body(): lax.psum_scatter(lax.dot_general(zpanel, plane, (((0,), (1,)), ((), ())),...  13.2 us
    all_gather x1, blocking collectives, body(): all_roots = lax.all_gather(roots, 'row', axis=0, tiled=True)  12.8 us
    all_to_all x1, blocking collectives, body(): lax.all_to_all(pieces, ('row', 'half'), split_axis=0, concat_axis=0, tile...  11.2 us
    psum x1, blocking collectives, body(): norms = lax.psum(jnp.sum(cauchy * cauchy, axis=0), ('col', 'half'))  5.66 us
  transfers between devices with their start and end apart: 1, of which 1 were waited for; matrix products, arithmetic and copies ran while one was open for 0% of the time, Pallas kernels for 0%

commit v1 on v0

v1 whole, which is shorter than its diff:
```python
import functools

import jax
import jax.numpy as jnp
from jax import lax
from jax.experimental import pallas as pl
from jax.experimental.pallas import tpu as pltpu
from jax.sharding import PartitionSpec as P

MESH = pl.DeviceIdType.MESH
LANES = 128


def kernel(dims, vecs, poles, weights, kept, roots, order, out,
           vbuf, rootbuf, theta, scaled, zbuf, acc, nacc, psend, precv, nsend, nrecv, asend, arecv,
           vsem, rsend, rrecv, pssem, prsem, nssem, nrsem, assem, arsem):
    n_row, n_col, n_half, cols, panel, block, sub = dims
    grp, row, col, half = (lax.axis_index(a) for a in ("grp", "row", "col", "half"))
    share = panel // n_col
    width = panel // n_row
    nrows = vbuf.shape[0]
    groups = n_row * n_half
    depth = nrows // groups
    n_blocks = cols // block

    def load(i):
        at = pl.ds(pl.multiple_of(i * block, block), block)
        return pltpu.make_async_copy(vecs.at[0, :, at], vbuf.at[:, at], vsem.at[i])

    for i in range(n_blocks):
        load(i).start()

    me = row * n_half + half
    barrier = pltpu.get_barrier_semaphore()
    for o in range(1, groups):
        g = lax.rem(me + o, groups)
        pl.semaphore_signal(barrier, inc=1, device_id=(grp, g // n_half, col, lax.rem(g, n_half)), device_id_type=MESH)
    for t in range(1, n_col):
        for h in range(n_half):
            pl.semaphore_signal(barrier, inc=1, device_id=(grp, row, lax.rem(col + t, n_col), h), device_id_type=MESH)

    scaled[...] = weights[...] * kept[...].astype(jnp.float32)
    order_col = jnp.transpose(jnp.broadcast_to(order[...], (8, panel)))[:, :1]

    pl.semaphore_wait(barrier, groups - 1 + (n_col - 1) * n_half)

    def root_copy(o):
        return pltpu.make_async_remote_copy(
            src_ref=roots, dst_ref=rootbuf.at[o], send_sem=rsend.at[o], recv_sem=rrecv.at[o],
            device_id=(grp, lax.rem(row + o, n_row), col, half), device_id_type=MESH)

    for o in range(1, n_row):
        root_copy(o).start()
    lane = lax.broadcasted_iota(jnp.int32, (panel, width), 1)
    picked = jnp.zeros((panel, width), jnp.float32)
    for o in range(n_row):
        if o:
            root_copy(o).wait()
        source = lax.rem(row + n_row - o, n_row)
        block_roots = rootbuf[o] if o else roots[...]
        picked = jnp.where(order_col - source * width == lane, block_roots, picked)
    theta[...] = jnp.broadcast_to(jnp.sum(picked, axis=1, keepdims=True), (panel, LANES))

    def chunk(t):
        base = pl.multiple_of(lax.rem(col + t, n_col) * share, share)
        acc[...] = jnp.zeros_like(acc)
        nacc[...] = jnp.zeros_like(nacc)

        def step(i, carry):
            if t == 1 or n_col == 1:
                load(i).wait()
            start = pl.multiple_of(i * block, block)
            total = acc[...]
            for s in range(block // sub):
                for k in range(0, share, 16):
                    th = theta[pl.ds(base + k, 16), :]
                    squares = nacc[k:k + 16, :]
                    for c in range(s * sub, (s + 1) * sub, LANES):
                        at = pl.ds(start + c, LANES)
                        cauchy = scaled[:, at] / (poles[:, at] - th)
                        squares += cauchy * cauchy
                        zbuf[k:k + 16, c:c + LANES] = cauchy.astype(jnp.bfloat16)
                    nacc[k:k + 16, :] = squares
                total += lax.dot_general(
                    vbuf[:, pl.ds(start + s * sub, sub)], zbuf[:, s * sub:(s + 1) * sub],
                    (((1,), (1,)), ((), ())), preferred_element_type=jnp.float32)
            acc[...] = total
            return carry

        lax.fori_loop(0, n_blocks, step, 0)
        nsend[t] = jnp.sum(jnp.transpose(nacc[...]), axis=0, keepdims=True)

    def norm_copy(t, o):
        return pltpu.make_async_remote_copy(
            src_ref=nsend.at[t], dst_ref=nrecv.at[t, o], send_sem=nssem.at[t, o], recv_sem=nrsem.at[t, o],
            device_id=(grp, row, lax.rem(col + t, n_col), lax.rem(half + o, n_half)), device_id_type=MESH)

    def part_copy(t):
        return pltpu.make_async_remote_copy(
            src_ref=psend.at[t - 1], dst_ref=precv.at[t - 1], send_sem=pssem.at[t - 1], recv_sem=prsem.at[t - 1],
            device_id=(grp, row, lax.rem(col + t, n_col), half), device_id_type=MESH)

    def piece_copy(o):
        g = lax.rem(me + o, groups)
        return pltpu.make_async_remote_copy(
            src_ref=asend.at[g], dst_ref=arecv.at[o], send_sem=assem.at[o], recv_sem=arsem.at[o],
            device_id=(grp, g // n_half, col, lax.rem(g, n_half)), device_id_type=MESH)

    norm_copies = [(t, o) for t in range(n_col) for o in range(n_half) if t or o]
    for t in range(1, n_col):
        chunk(t)
        psend[t - 1] = acc[...].astype(jnp.bfloat16)
        part_copy(t).start()
        for o in range(n_half):
            norm_copy(t, o).start()
    chunk(0)
    for o in range(1, n_half):
        norm_copy(0, o).start()
    total = acc[...]
    for t in range(1, n_col):
        part_copy(t).wait()
        total += precv[t - 1].astype(jnp.float32)
    asend[...] = total.reshape(groups, depth, share).astype(jnp.bfloat16)
    for o in range(1, groups):
        piece_copy(o).start()
    norms = nsend[0]
    for t, o in norm_copies:
        norm_copy(t, o).wait()
        norms += nrecv[t, o]
    scale = lax.rsqrt(norms + 1e-06)
    for o in range(groups):
        if o:
            piece_copy(o).wait()
        g = lax.rem(me + groups - o, groups)
        piece = arecv[o] if o else asend[me]
        out[0, g // n_half, lax.rem(g, n_half)] = (piece.astype(jnp.float32) * scale).astype(jnp.bfloat16)


def body(vecs, poles, weights, kept, roots, order):
    n_row, n_col, n_half = (lax.axis_size(a) for a in ("row", "col", "half"))
    nrows, cols = vecs.shape[1:]
    panel = order.shape[0]
    share, groups = panel // n_col, n_row * n_half
    depth = nrows // groups
    block = min(2048, cols)
    sub = min(512, block)
    vmem = pl.BlockSpec(memory_space=pltpu.VMEM)
    dma = pltpu.SemaphoreType.DMA
    others = max(n_col - 1, 1)
    return pl.pallas_call(
        functools.partial(kernel, (n_row, n_col, n_half, cols, panel, block, sub)),
        out_shape=jax.ShapeDtypeStruct((1, n_row, n_half, depth, share), jnp.bfloat16),
        in_specs=[pl.BlockSpec(memory_space=pl.ANY)] + [vmem] * 5,
        out_specs=vmem,
        scratch_shapes=[
            pltpu.VMEM((nrows, cols), jnp.bfloat16),
            pltpu.VMEM((n_row, 1, panel // n_row), jnp.float32),
            pltpu.VMEM((panel, LANES), jnp.float32),
            pltpu.VMEM((1, cols), jnp.float32),
            pltpu.VMEM((share, block), jnp.bfloat16),
            pltpu.VMEM((nrows, share), jnp.float32),
            pltpu.VMEM((share, LANES), jnp.float32),
            pltpu.VMEM((others, nrows, share), jnp.bfloat16),
            pltpu.VMEM((others, nrows, share), jnp.bfloat16),
            pltpu.VMEM((n_col, 1, share), jnp.float32),
            pltpu.VMEM((n_col, n_half, 1, share), jnp.float32),
            pltpu.VMEM((groups, depth, share), jnp.bfloat16),
            pltpu.VMEM((groups, depth, share), jnp.bfloat16),
            dma((cols // block,)),
            dma((n_row,)),
            dma((n_row,)),
            dma((others,)),
            dma((others,)),
            dma((n_col, n_half)),
            dma((n_col, n_half)),
            dma((groups,)),
            dma((groups,)),
        ],
        compiler_params=pltpu.CompilerParams(collective_id=0, has_side_effects=True),
        name="merge",
    )(vecs, poles, weights, kept, roots[None, :], order[None, :])


def solution(mesh):
    return jax.shard_map(
        body,
        mesh=mesh,
        in_specs=(
            P(("grp", "half"), "row", "col"),
            P(("grp", "half"), "col"),
            P(("grp", "half"), "col"),
            P(("grp", "half"), "col"),
            P(("grp", "row")),
            P("grp"),
        ),
        out_specs=P(("grp", "row", "half"), None, None, None, "col"),
        check_vma=False,
    )
```

time: 88.3 us -> 31 us (0.35)
  blocking collectives: 29.6 us -> 0 us
  Pallas kernels: 0 us -> 29.2 us
  other arithmetic: 15.7 us -> 0 us
  matrix products: 15.2 us -> 0 us
  between operations: 13.4 us -> 0.01 us
  waiting for transfers between devices: 13.2 us -> 0 us
    pallas_call x0 -> x1, Pallas kernels: none -> 29.2 us  [body(): pl.pallas_call(functools.partial(kernel, (n_row, n_col, n_half, cols, pan...]
    dot_general x2 -> x0, matrix products: 15.2 us -> none  [the longest x1 13.9 us: body(): lax.dot_general(zpanel, plane, (((0,), (1,)), ((), ())), preferred_elemen...]
    reduce_sum x1 -> x0, other arithmetic: 13.8 us -> none  [body(): norms = lax.psum(jnp.sum(cauchy * cauchy, axis=0), ('col', 'half'))]
    reduce_scatter x1 -> x0, waiting for transfers between devices: 13.2 us -> none  [body(): lax.psum_scatter(lax.dot_general(zpanel, plane, (((0,), (1,)), ((), ())),...]
    all_gather x1 -> x0, blocking collectives: 12.8 us -> none  [body(): all_roots = lax.all_gather(roots, 'row', axis=0, tiled=True)]
    all_to_all x1 -> x0, blocking collectives: 11.2 us -> none  [body(): lax.all_to_all(pieces, ('row', 'half'), split_axis=0, concat_axis=0, tile...]
    psum x1 -> x0, blocking collectives: 5.66 us -> none  [body(): norms = lax.psum(jnp.sum(cauchy * cauchy, axis=0), ('col', 'half'))]
    transpose x1 -> x0, other arithmetic: 0.96 us -> none  [body(): block = jnp.transpose(share.astype(jnp.bfloat16))]
  transfers between devices with their start and end apart: 1 -> 0, of which waited for: 1 -> 0; matrix products, arithmetic and copies ran while one was open for 0% -> 0% of each run, Pallas kernels for 0% -> 0%
where the time goes in v1:
time: 31 us; the launch traced here: 30.8 us
  Pallas kernels  29.2 us (94%)
  local copies, waits for them, and re-layouts  1.57 us (5%)
    pallas_call x1, Pallas kernels, body(): pl.pallas_call(functools.partial(kernel, (n_row, n_col, n_half, cols, pan...  29.2 us
    unnamed x1, local copies, waits for them, and re-layouts  1.57 us

profile of v1, /device:TPU:0, one launch (start us, length us, event | category | flops | bytes accessed | tf_op | source)
XLA Modules:
  0.0 30.8 jit_solution(13324475243535279510)
XLA Ops:
  0.0 29.2 %merge.1 = bf16[1,4,2,32,256]{4,3,2,1,0:T(8,128)(2,1)} custom-call(bf16[1,256,16384]{2,1,0:T(8,128)(2,1)} %vecs.1, f32[1,16384]{1,0:T(1,128)} %poles.1, f32[1,16384]{1,0:T(1,128)} %weights.1, s32[1,16384]{1,0:T(1,128)} %kept.1, f32[1,128]{1,0:T(1,128)} %bitcast.3, s32[1,512]{1,0:T(1,128)} %bitcast.2), custom_call_target="tpu_custom_call" | custom-call | tf_op jit(solution)/shard_map/merge/pallas_call | solution.py:150
  29.2 1.6 %copy.8 = bf16[1,4,2,32,256]{4,3,2,1,0:T(8,128)(2,1)} copy(bf16[1,4,2,32,256]{4,3,2,1,0:T(8,128)(2,1)} %merge.1) | data formatting | bytes 262144

commit v2 on v1

--- a/solution.py
+++ b/solution.py
@@ -18,17 +18,20 @@
     grp, row, col, half = (lax.axis_index(a) for a in ("grp", "row", "col", "half"))
     share = panel // n_col
     width = panel // n_row
-    nrows = vbuf.shape[0]
+    nrows = vbuf.shape[1]
     groups = n_row * n_half
     depth = nrows // groups
     n_blocks = cols // block
 
-    def load(i):
-        at = pl.ds(pl.multiple_of(i * block, block), block)
-        return pltpu.make_async_copy(vecs.at[0, :, at], vbuf.at[:, at], vsem.at[i])
-
-    for i in range(n_blocks):
-        load(i).start()
+    tiles = block // LANES
+
+    def tile_load(i, j):
+        at = pl.ds(pl.multiple_of(i * block + j * LANES, LANES), LANES)
+        return pltpu.make_async_copy(vecs.at[0, :, at], vbuf.at[i * tiles + j], vsem.at[i])
+
+    def loaded(i):
+        here = vbuf.at[pl.ds(i * tiles, tiles)]
+        pltpu.make_async_copy(here, here, vsem.at[i]).wait()
 
     me = row * n_half + half
     barrier = pltpu.get_barrier_semaphore()
@@ -39,6 +42,9 @@
         for h in range(n_half):
             pl.semaphore_signal(barrier, inc=1, device_id=(grp, row, lax.rem(col + t, n_col), h), device_id_type=MESH)
 
+    for i in range(n_blocks):
+        for j in range(tiles):
+            tile_load(i, j).start()
     scaled[...] = weights[...] * kept[...].astype(jnp.float32)
     order_col = jnp.transpose(jnp.broadcast_to(order[...], (8, panel)))[:, :1]
 
@@ -68,7 +74,7 @@
 
         def step(i, carry):
             if t == 1 or n_col == 1:
-                load(i).wait()
+                loaded(i)
             start = pl.multiple_of(i * block, block)
             total = acc[...]
             for s in range(block // sub):
@@ -79,10 +85,12 @@
                         at = pl.ds(start + c, LANES)
                         cauchy = scaled[:, at] / (poles[:, at] - th)
                         squares += cauchy * cauchy
-                        zbuf[k:k + 16, c:c + LANES] = cauchy.astype(jnp.bfloat16)
+                        zbuf[c // LANES, k:k + 16, :] = cauchy.astype(jnp.bfloat16)
                     nacc[k:k + 16, :] = squares
+                tile = range(s * sub // LANES, (s + 1) * sub // LANES)
                 total += lax.dot_general(
-                    vbuf[:, pl.ds(start + s * sub, sub)], zbuf[:, s * sub:(s + 1) * sub],
+                    jnp.concatenate([vbuf[i * tiles + j] for j in tile], axis=1),
+                    jnp.concatenate([zbuf[j] for j in tile], axis=1),
                     (((1,), (1,)), ((), ())), preferred_element_type=jnp.float32)
             acc[...] = total
             return carry
@@ -153,11 +161,11 @@
         in_specs=[pl.BlockSpec(memory_space=pl.ANY)] + [vmem] * 5,
         out_specs=vmem,
         scratch_shapes=[
-            pltpu.VMEM((nrows, cols), jnp.bfloat16),
+            pltpu.VMEM((cols // LANES, nrows, LANES), jnp.bfloat16),
             pltpu.VMEM((n_row, 1, panel // n_row), jnp.float32),
             pltpu.VMEM((panel, LANES), jnp.float32),
             pltpu.VMEM((1, cols), jnp.float32),
-            pltpu.VMEM((share, block), jnp.bfloat16),
+            pltpu.VMEM((block // LANES, share, LANES), jnp.bfloat16),
             pltpu.VMEM((nrows, share), jnp.float32),
             pltpu.VMEM((share, LANES), jnp.float32),
             pltpu.VMEM((others, nrows, share), jnp.bfloat16),

time: 31 us -> 29.1 us (0.939)
  Pallas kernels: 29.2 us -> 27.3 us
    pallas_call x1, Pallas kernels: 29.2 us -> 27.3 us  [body(): pl.pallas_call(functools.partial(kernel, (n_row, n_col, n_half, cols, pan...]
where the time goes in v2:
time: 29.1 us; the launch traced here: 28.9 us
  Pallas kernels  27.3 us (94%)
  local copies, waits for them, and re-layouts  1.57 us (5%)
    pallas_call x1, Pallas kernels, body(): pl.pallas_call(functools.partial(kernel, (n_row, n_col, n_half, cols, pan...  27.3 us
    unnamed x1, local copies, waits for them, and re-layouts  1.57 us

profile of v2, /device:TPU:0, one launch (start us, length us, event | category | flops | bytes accessed | tf_op | source)
XLA Modules:
  0.0 28.9 jit_solution(6113207404486130133)
XLA Ops:
  0.0 27.3 %merge.1 = bf16[1,4,2,32,256]{4,3,2,1,0:T(8,128)(2,1)} custom-call(bf16[1,256,16384]{2,1,0:T(8,128)(2,1)} %vecs.1, f32[1,16384]{1,0:T(1,128)} %poles.1, f32[1,16384]{1,0:T(1,128)} %weights.1, s32[1,16384]{1,0:T(1,128)} %kept.1, f32[1,128]{1,0:T(1,128)} %bitcast.3, s32[1,512]{1,0:T(1,128)} %bitcast.2), custom_call_target="tpu_custom_call" | custom-call | tf_op jit(solution)/shard_map/merge/pallas_call | solution.py:158
  27.3 1.6 %copy.8 = bf16[1,4,2,32,256]{4,3,2,1,0:T(8,128)(2,1)} copy(bf16[1,4,2,32,256]{4,3,2,1,0:T(8,128)(2,1)} %merge.1) | data formatting | bytes 262144

commit v3 on v2

--- a/solution.py
+++ b/solution.py
@@ -12,9 +12,9 @@
 
 
 def kernel(dims, vecs, poles, weights, kept, roots, order, out,
-           vbuf, rootbuf, theta, scaled, zbuf, acc, nacc, psend, precv, nsend, nrecv, asend, arecv,
-           vsem, rsend, rrecv, pssem, prsem, nssem, nrsem, assem, arsem):
-    n_row, n_col, n_half, cols, panel, block, sub = dims
+           vbuf, rootbuf, theta, scaled, picks, raw, mask, centers, own, zeven, zodd, acc, nacc, psend, precv, nsend, nrecv, asend, arecv,
+           ssem, vsem, rsend, rrecv, pssem, prsem, nssem, nrsem, assem, arsem):
+    n_row, n_col, n_half, cols, panel, block, rows = dims
     grp, row, col, half = (lax.axis_index(a) for a in ("grp", "row", "col", "half"))
     share = panel // n_col
     width = panel // n_row
@@ -42,12 +42,16 @@
         for h in range(n_half):
             pl.semaphore_signal(barrier, inc=1, device_id=(grp, row, lax.rem(col + t, n_col), h), device_id_type=MESH)
 
+    small = [(order, picks), (weights, raw), (kept, mask), (poles, centers), (roots, own)]
+    fetches = [pltpu.make_async_copy(src, dst, ssem.at[n]) for n, (src, dst) in enumerate(small)]
+    for fetch in fetches:
+        fetch.start()
+
     for i in range(n_blocks):
         for j in range(tiles):
             tile_load(i, j).start()
-    scaled[...] = weights[...] * kept[...].astype(jnp.float32)
-    order_col = jnp.transpose(jnp.broadcast_to(order[...], (8, panel)))[:, :1]
-
+    acc[...] = jnp.zeros_like(acc)
+    zodd[...] = jnp.zeros_like(zodd)
     pl.semaphore_wait(barrier, groups - 1 + (n_col - 1) * n_half)
 
     def root_copy(o):
@@ -57,45 +61,76 @@
 
     for o in range(1, n_row):
         root_copy(o).start()
+    for fetch in fetches:
+        fetch.wait()
+    scaled[...] = raw[...] * mask[...].astype(jnp.float32)
+    wanted = jnp.transpose(jnp.broadcast_to(picks[...], (LANES, panel)))[:, :width]
     lane = lax.broadcasted_iota(jnp.int32, (panel, width), 1)
     picked = jnp.zeros((panel, width), jnp.float32)
     for o in range(n_row):
         if o:
             root_copy(o).wait()
         source = lax.rem(row + n_row - o, n_row)
-        block_roots = rootbuf[o] if o else roots[...]
-        picked = jnp.where(order_col - source * width == lane, block_roots, picked)
+        picked = jnp.where(wanted - source * width == lane, rootbuf[o] if o else own[...], picked)
     theta[...] = jnp.broadcast_to(jnp.sum(picked, axis=1, keepdims=True), (panel, LANES))
 
+    strips = share // rows
+    span = tiles // strips
+
+    def dot(z, i, k):
+        acc[...] += lax.dot_general(
+            jnp.concatenate([vbuf[i * tiles + k * span + j] for j in range(span)], axis=1),
+            jnp.concatenate([z[k * span + j] for j in range(span)], axis=1),
+            (((1,), (1,)), ((), ())), preferred_element_type=jnp.float32)
+
     def chunk(t):
-        base = pl.multiple_of(lax.rem(col + t, n_col) * share, share)
-        acc[...] = jnp.zeros_like(acc)
+        base = lax.rem(col + t, n_col) * share
         nacc[...] = jnp.zeros_like(nacc)
 
-        def step(i, carry):
+        def fill(z, i, k):
+            first = pl.multiple_of(k * rows, rows)
+            th = [theta[pl.ds(pl.multiple_of(base + k * rows + r, 16), 16), :] for r in range(0, rows, 16)]
+            squares = [nacc[pl.ds(first + r, 16), :] for r in range(0, rows, 16)]
+            for j in range(tiles):
+                at = pl.ds(pl.multiple_of(i * block + j * LANES, LANES), LANES)
+                weight, center = scaled[:, at], centers[:, at]
+                for n in range(rows // 16):
+                    cauchy = weight / (center - th[n])
+                    squares[n] += cauchy * cauchy
+                    z[j, pl.ds(first + n * 16, 16), :] = cauchy.astype(jnp.bfloat16)
+            for n in range(rows // 16):
+                nacc[pl.ds(first + n * 16, 16), :] = squares[n]
+
+        def pair(p, carry):
+            def even(k, carry):
+                dot(zodd, jnp.maximum(2 * p - 1, 0), k)
+                fill(zeven, 2 * p, k)
+                return carry
+
+            def odd(k, carry):
+                dot(zeven, 2 * p, k)
+                fill(zodd, 2 * p + 1, k)
+                return carry
+
             if t == 1 or n_col == 1:
-                loaded(i)
-            start = pl.multiple_of(i * block, block)
-            total = acc[...]
-            for s in range(block // sub):
-                for k in range(0, share, 16):
-                    th = theta[pl.ds(base + k, 16), :]
-                    squares = nacc[k:k + 16, :]
-                    for c in range(s * sub, (s + 1) * sub, LANES):
-                        at = pl.ds(start + c, LANES)
-                        cauchy = scaled[:, at] / (poles[:, at] - th)
-                        squares += cauchy * cauchy
-                        zbuf[c // LANES, k:k + 16, :] = cauchy.astype(jnp.bfloat16)
-                    nacc[k:k + 16, :] = squares
-                tile = range(s * sub // LANES, (s + 1) * sub // LANES)
-                total += lax.dot_general(
-                    jnp.concatenate([vbuf[i * tiles + j] for j in tile], axis=1),
-                    jnp.concatenate([zbuf[j] for j in tile], axis=1),
-                    (((1,), (1,)), ((), ())), preferred_element_type=jnp.float32)
-            acc[...] = total
+                loaded(2 * p)
+                loaded(2 * p + 1)
+            lax.fori_loop(0, strips, even, 0)
+
+            @pl.when(p == 0)
+            def _():
+                acc[...] = jnp.zeros_like(acc)
+
+            lax.fori_loop(0, strips, odd, 0)
             return carry
 
-        lax.fori_loop(0, n_blocks, step, 0)
+        lax.fori_loop(0, n_blocks // 2, pair, 0)
+
+        def rest(k, carry):
+            dot(zodd, n_blocks - 1, k)
+            return carry
+
+        lax.fori_loop(0, strips, rest, 0)
         nsend[t] = jnp.sum(jnp.transpose(nacc[...]), axis=0, keepdims=True)
 
     def norm_copy(t, o):
@@ -150,21 +185,27 @@
     panel = order.shape[0]
     share, groups = panel // n_col, n_row * n_half
     depth = nrows // groups
-    block = min(2048, cols)
-    sub = min(512, block)
+    block = min(4096, cols // 2)
+    rows = min(128, share)
     vmem = pl.BlockSpec(memory_space=pltpu.VMEM)
     dma = pltpu.SemaphoreType.DMA
     others = max(n_col - 1, 1)
     return pl.pallas_call(
-        functools.partial(kernel, (n_row, n_col, n_half, cols, panel, block, sub)),
+        functools.partial(kernel, (n_row, n_col, n_half, cols, panel, block, rows)),
         out_shape=jax.ShapeDtypeStruct((1, n_row, n_half, depth, share), jnp.bfloat16),
-        in_specs=[pl.BlockSpec(memory_space=pl.ANY)] + [vmem] * 5,
+        in_specs=[pl.BlockSpec(memory_space=pl.ANY)] * 6,
         out_specs=vmem,
         scratch_shapes=[
             pltpu.VMEM((cols // LANES, nrows, LANES), jnp.bfloat16),
             pltpu.VMEM((n_row, 1, panel // n_row), jnp.float32),
             pltpu.VMEM((panel, LANES), jnp.float32),
             pltpu.VMEM((1, cols), jnp.float32),
+            pltpu.VMEM((1, panel), jnp.int32),
+            pltpu.VMEM((1, cols), jnp.float32),
+            pltpu.VMEM((1, cols), jnp.int32),
+            pltpu.VMEM((1, cols), jnp.float32),
+            pltpu.VMEM((1, panel // n_row), jnp.float32),
+            pltpu.VMEM((block // LANES, share, LANES), jnp.bfloat16),
             pltpu.VMEM((block // LANES, share, LANES), jnp.bfloat16),
             pltpu.VMEM((nrows, share), jnp.float32),
             pltpu.VMEM((share, LANES), jnp.float32),
@@ -174,6 +215,7 @@
             pltpu.VMEM((n_col, n_half, 1, share), jnp.float32),
             pltpu.VMEM((groups, depth, share), jnp.bfloat16),
             pltpu.VMEM((groups, depth, share), jnp.bfloat16),
+            dma((5,)),
             dma((cols // block,)),
             dma((n_row,)),
             dma((n_row,)),

time: 29.1 us -> 25.7 us (0.88)
  Pallas kernels: 27.3 us -> 24 us
    pallas_call x1, Pallas kernels: 27.3 us -> 24 us  [body(): pl.pallas_call(functools.partial(kernel, (n_row, n_col, n_half, cols, pan...]
where the time goes in v3:
time: 25.7 us; the launch traced here: 25.6 us
  Pallas kernels  24 us (93%)
  local copies, waits for them, and re-layouts  1.57 us (6%)
    pallas_call x1, Pallas kernels, body(): pl.pallas_call(functools.partial(kernel, (n_row, n_col, n_half, cols, pan...  24 us
    unnamed x1, local copies, waits for them, and re-layouts  1.57 us

profile of v3, /device:TPU:0, one launch (start us, length us, event | category | flops | bytes accessed | tf_op | source)
XLA Modules:
  0.0 25.6 jit_solution(13393913637595145831)
XLA Ops:
  0.0 24.0 %merge.1 = bf16[1,4,2,32,256]{4,3,2,1,0:T(8,128)(2,1)} custom-call(bf16[1,256,16384]{2,1,0:T(8,128)(2,1)} %vecs.1, f32[1,16384]{1,0:T(1,128)} %poles.1, f32[1,16384]{1,0:T(1,128)} %weights.1, s32[1,16384]{1,0:T(1,128)} %kept.1, f32[1,128]{1,0:T(1,128)} %bitcast.3, s32[1,512]{1,0:T(1,128)} %bitcast.2), custom_call_target="tpu_custom_call" | custom-call | tf_op jit(solution)/shard_map/merge/pallas_call | solution.py:193
  24.0 1.6 %copy.8 = bf16[1,4,2,32,256]{4,3,2,1,0:T(8,128)(2,1)} copy(bf16[1,4,2,32,256]{4,3,2,1,0:T(8,128)(2,1)} %merge.1) | data formatting | bytes 262144

commit v4 on v3

--- a/solution.py
+++ b/solution.py
@@ -164,14 +164,15 @@
         part_copy(t).wait()
         total += precv[t - 1].astype(jnp.float32)
     asend[...] = total.reshape(groups, depth, share).astype(jnp.bfloat16)
-    for o in range(1, groups):
+    far_first = sorted(range(1, groups), key=lambda o: -min(o // n_half, n_row - o // n_half))
+    for o in far_first:
         piece_copy(o).start()
     norms = nsend[0]
     for t, o in norm_copies:
         norm_copy(t, o).wait()
         norms += nrecv[t, o]
     scale = lax.rsqrt(norms + 1e-06)
-    for o in range(groups):
+    for o in [0] + far_first[::-1]:
         if o:
             piece_copy(o).wait()
         g = lax.rem(me + groups - o, groups)

time: 25.7 us -> 26.1 us (1.016)
  Pallas kernels: 24 us -> 24.3 us
    pallas_call x1, Pallas kernels: 24 us -> 24.3 us  [body(): pl.pallas_call(functools.partial(kernel, (n_row, n_col, n_half, cols, pan...]
where the time goes in v4:
time: 26.1 us; the launch traced here: 25.9 us
  Pallas kernels  24.3 us (93%)
  local copies, waits for them, and re-layouts  1.57 us (6%)
    pallas_call x1, Pallas kernels, body(): pl.pallas_call(functools.partial(kernel, (n_row, n_col, n_half, cols, pan...  24.3 us
    unnamed x1, local copies, waits for them, and re-layouts  1.57 us

profile of v4, /device:TPU:0, one launch (start us, length us, event | category | flops | bytes accessed | tf_op | source)
XLA Modules:
  0.0 25.9 jit_solution(2103272206435863097)
XLA Ops:
  0.0 24.3 %merge.1 = bf16[1,4,2,32,256]{4,3,2,1,0:T(8,128)(2,1)} custom-call(bf16[1,256,16384]{2,1,0:T(8,128)(2,1)} %vecs.1, f32[1,16384]{1,0:T(1,128)} %poles.1, f32[1,16384]{1,0:T(1,128)} %weights.1, s32[1,16384]{1,0:T(1,128)} %kept.1, f32[1,128]{1,0:T(1,128)} %bitcast.3, s32[1,512]{1,0:T(1,128)} %bitcast.2), custom_call_target="tpu_custom_call" | custom-call | tf_op jit(solution)/shard_map/merge/pallas_call | solution.py:194
  24.4 1.6 %copy.8 = bf16[1,4,2,32,256]{4,3,2,1,0:T(8,128)(2,1)} copy(bf16[1,4,2,32,256]{4,3,2,1,0:T(8,128)(2,1)} %merge.1) | data formatting | bytes 262144
